TPU v7x, 32 devices: a whole 2x2x4 slice. The times are simulated.
32 devices in a mesh: groups: 2 (over x), hit: 8 (over z, y), query: 2 (over core).
Axes of the slice: x: 2, y: 2, z: 4, core: 2. Of those that a mesh axis runs over, the one named last changes fastest.
Arguments:
- hits: bfloat16 [16384, 512], P(('groups', 'hit', 'query')), parts along dimension 0, may hold values from -24 to 24
- order: int32 [32, 512], P(('groups', 'hit', 'query')), parts along dimension 0, may hold values from 0 to 511, each once within a row
- valid: int32 [16384], P(('groups', 'hit', 'query')), parts along dimension 0, may hold values 0 or 1
- reach: int32 [16384], P(('groups', 'hit', 'query')), parts along dimension 0, may hold values from 128 to 512, as said below
- enc_wq: bfloat16 [512, 512], replicated, may hold values from -3 to 3
- enc_wk: bfloat16 [512, 512], replicated, may hold values from -1 to 1
- enc_wv: bfloat16 [512, 512], replicated, may hold values from -0.25 to 0.25
- enc_wo: bfloat16 [512, 512], replicated, may hold values from -0.25 to 0.25
- enc_gain1: float32 [512], replicated, may hold values from 0.5 to 1.5
- ffn_up: bfloat16 [512, 2048], replicated, may hold values from -0.25 to 0.25
- ffn_down: bfloat16 [2048, 512], replicated, may hold values from -0.125 to 0.125
- enc_gain2: float32 [512], replicated, may hold values from 0.5 to 1.5
- object_queries: bfloat16 [512, 512], P(('groups', 'hit', 'query')), parts along dimension 0, may hold values from -48 to 48
- dec_wq: bfloat16 [512, 512], replicated, may hold values from -8 to 8
- dec_wk: bfloat16 [512, 512], replicated, may hold values from -0.25 to 0.25
- dec_wv: bfloat16 [512, 512], replicated, may hold values from -0.25 to 0.25
- dec_wo: bfloat16 [512, 512], replicated, may hold values from -0.25 to 0.25
- dec_gain: float32 [512], replicated, may hold values from 0.5 to 1.5
- out_proj: bfloat16 [512, 512], replicated, may hold values from -0.25 to 0.25
Outputs:
- encoded: bfloat16 [16384, 512], P(('groups', 'hit', 'query')), parts along dimension 0
- decoded: bfloat16 [512, 512], P(('groups', 'hit', 'query')), parts along dimension 0
There are 2 independent parts, one for each index of `groups`. A program takes and returns all parts, laid end to end along the dimension named above; an argument that names none is the same for every part. Nothing has to cross between parts.
Inputs may be any that keep to these rules, and one draw needn't show every extreme that they name: The first hit of every block of 512 arrival positions has reach 512.
All inputs are finite; a program needn't handle non-finite values. No bound on the sum of `valid` on one device may be relied on, other than what follows from the above.
Results may differ from a plain program's by a relative error of at most 0.035.
Values may be sent and summed in bfloat16 or wider, within the bound.
No kernel may reach another device: no remote copies, remote signals or barrier semaphores. Data moves between devices by JAX's collectives and lax.ppermute only.
A program may use at most 192 MiB of HBM per device.

v0:
```python
import math
import jax
import jax.numpy as jnp
from jax import lax
from jax.sharding import PartitionSpec as P

D = 512
HEADS = 8
WINDOW = 512


def padded(cells, sides, width):
    for axis, dim in sides:
        count = lax.axis_size(axis)
        head = lax.slice_in_dim(cells, 0, width, axis=dim)
        tail = lax.slice_in_dim(cells, cells.shape[dim] - width, cells.shape[dim], axis=dim)
        cells = jnp.concatenate(
            [
                lax.ppermute(tail, axis, [(i, (i + 1) % count) for i in range(count)]),
                cells,
                lax.ppermute(head, axis, [((i + 1) % count, i) for i in range(count)]),
            ],
            axis=dim,
        )
    return cells


def joined(value, axis, combine):
    everything = jax.tree.map(lambda part: lax.all_gather(part, axis), value)
    leading = jax.tree.map(lambda part: part[0], everything)

    def lap(k, so_far):
        return combine(so_far, jax.tree.map(lambda part: part[k], everything))

    return lax.fori_loop(1, lax.axis_size(axis), lap, leading)


def project(rows, weight):
    return jnp.dot(rows, weight, preferred_element_type=jnp.float32).astype(jnp.bfloat16)


def rms_norm(values, gain):
    scale = lax.rsqrt(jnp.mean(values * values, axis=-1, keepdims=True) + 1e-05)
    return values * scale * gain


def band_attention(queries, keys, values, key_valid, reach):
    count = queries.shape[0]
    span = keys.shape[0]
    margin = (span - count) // 2
    width = queries.shape[1] // HEADS
    query_heads = queries.reshape(count, HEADS, width)
    key_heads = keys.reshape(span, HEADS, width)
    value_heads = values.reshape(span, HEADS, width)
    scores = jnp.einsum(
        "qhd,khd->hqk", query_heads, key_heads, preferred_element_type=jnp.float32
    ) * (1.0 / math.sqrt(width))
    offset = jnp.arange(span, dtype=jnp.int32)[None, :] - (
        jnp.arange(count, dtype=jnp.int32)[:, None] + margin
    )
    allowed = (jnp.abs(offset) <= reach[:, None]) & ((key_valid[None, :] > 0) | (offset == 0))
    scores = jnp.where(allowed[None], scores, -jnp.inf)
    peak = jnp.max(scores, axis=2, keepdims=True)
    expo = jnp.where(allowed[None], jnp.exp(scores - peak), 0.0)
    probs = (expo / jnp.sum(expo, axis=2, keepdims=True)).astype(jnp.bfloat16)
    context = jnp.einsum("hqk,khd->qhd", probs, value_heads, preferred_element_type=jnp.float32)
    return context.reshape(count, HEADS * width).astype(jnp.bfloat16)


def encoder_tail(context, sorted_hits, enc_wo, enc_gain1, ffn_up, ffn_down, enc_gain2):
    attn_res = jnp.dot(context, enc_wo, preferred_element_type=jnp.float32) + sorted_hits.astype(
        jnp.float32
    )
    middle = rms_norm(attn_res, enc_gain1).astype(jnp.bfloat16)
    hidden = jax.nn.gelu(
        jnp.dot(middle, ffn_up, preferred_element_type=jnp.float32), approximate=True
    ).astype(jnp.bfloat16)
    ffn_res = jnp.dot(hidden, ffn_down, preferred_element_type=jnp.float32) + middle.astype(
        jnp.float32
    )
    return rms_norm(ffn_res, enc_gain2).astype(jnp.bfloat16)


def span_partial(queries, keys, values):
    count = queries.shape[0]
    span = keys.shape[0]
    width = queries.shape[1] // HEADS
    query_heads = queries.reshape(count, HEADS, width)
    key_heads = keys.reshape(span, HEADS, width)
    value_heads = values.reshape(span, HEADS, width)
    scores = jnp.einsum(
        "qhd,khd->qhk", query_heads, key_heads, preferred_element_type=jnp.float32
    ) * (1.0 / math.sqrt(width))
    peak = jnp.max(scores, axis=2)
    expo = jnp.exp(scores - peak[:, :, None])
    total = jnp.sum(expo, axis=2)
    weights = expo.astype(jnp.bfloat16)
    output = jnp.einsum("qhk,khd->qhd", weights, value_heads, preferred_element_type=jnp.float32)
    return (peak, total, output.reshape(count, HEADS * width))


def merge_partials(first, second):
    width = D // HEADS
    peak = jnp.maximum(first[0], second[0])
    left = jnp.exp(first[0] - peak)
    right = jnp.exp(second[0] - peak)
    total = first[1] * left + second[1] * right
    output = first[2] * jnp.repeat(left, width, axis=1) + second[2] * jnp.repeat(
        right, width, axis=1
    )
    return (peak, total, output)


def on_device(
    hits,
    order,
    valid,
    reach,
    enc_wq,
    enc_wk,
    enc_wv,
    enc_wo,
    enc_gain1,
    ffn_up,
    ffn_down,
    enc_gain2,
    object_queries,
    dec_wq,
    dec_wk,
    dec_wv,
    dec_wo,
    dec_gain,
    out_proj,
):
    rows = hits.shape[0]
    place = order[0]
    sorted_hits = hits[place]
    sorted_valid = valid[place].astype(jnp.bfloat16)
    sorted_reach = reach[place]
    queries = project(sorted_hits, enc_wq)
    wide_hits, wide_valid = (
        padded(sorted_hits, ((("hit", "query"), 0),), WINDOW),
        padded(sorted_valid, ((("hit", "query"), 0),), WINDOW),
    )
    wide_keys = project(wide_hits, enc_wk)
    wide_values = project(wide_hits, enc_wv)
    block = 512

    def attend(index):
        start = index * block
        return band_attention(queries, wide_keys, wide_values, wide_valid, sorted_reach)

    context = lax.map(attend, jnp.arange(rows // block, dtype=jnp.int32)).reshape(
        rows, queries.shape[1]
    )
    encoded = encoder_tail(context, sorted_hits, enc_wo, enc_gain1, ffn_up, ffn_down, enc_gain2)
    local_queries = project(object_queries, dec_wq)
    span_keys, span_values = (
        lax.all_gather(project(encoded, dec_wk), "query", axis=0, tiled=True),
        lax.all_gather(project(encoded, dec_wv), "query", axis=0, tiled=True),
    )
    all_queries = lax.all_gather(local_queries, "hit", axis=0, tiled=True)
    count = all_queries.shape[0]
    qblock = 512 if count % 512 == 0 else count

    def partial_block(index):
        return span_partial(all_queries, span_keys, span_values)

    peaks, totals, outputs = lax.map(partial_block, jnp.arange(count // qblock, dtype=jnp.int32))
    width = D // HEADS
    peaks = peaks.reshape(count, HEADS)
    totals = totals.reshape(count, HEADS)
    outputs = outputs.reshape(count, HEADS * width)
    owned = object_queries.shape[0]
    highest, merged_total, merged_out = joined((peaks, totals, outputs), "hit", merge_partials)
    start = lax.axis_index("hit") * owned
    numer = lax.dynamic_slice_in_dim(merged_out, start, owned, 0)
    denom = lax.dynamic_slice_in_dim(merged_total, start, owned, 0)
    cross = (numer / jnp.repeat(denom, width, axis=1)).astype(jnp.bfloat16)
    dec_res = jnp.dot(cross, dec_wo, preferred_element_type=jnp.float32) + object_queries.astype(
        jnp.float32
    )
    normed = rms_norm(dec_res, dec_gain).astype(jnp.bfloat16)
    decoded = jnp.dot(normed, out_proj, preferred_element_type=jnp.float32).astype(jnp.bfloat16)
    return (encoded, decoded)


def solution(mesh):
    in_specs = (
        P(("groups", "hit", "query"), None),
        P(("groups", "hit", "query"), None),
        P(("groups", "hit", "query")),
        P(("groups", "hit", "query")),
        P(),
        P(),
        P(),
        P(),
        P(),
        P(),
        P(),
        P(),
        P(("groups", "hit", "query"), None),
        P(),
        P(),
        P(),
        P(),
        P(),
        P(),
    )
    out_specs = (P(("groups", "hit", "query"), None), P(("groups", "hit", "query"), None))
    return jax.shard_map(
        on_device, mesh=mesh, in_specs=in_specs, out_specs=out_specs, check_vma=False
    )
```

profile of v0, /device:TPU:0, one launch (start us, length us, event | category | flops | bytes accessed | tf_op | source)
XLA Modules:
  0.0 208.7 jit_solution(11262240188574677869)
XLA Ops:
  8.1 3.1 %gather_fusion = bf16[512,512]{1,0:T(8,128)(2,1)S(1)} fusion(bf16[512,512]{1,0:T(8,128)(2,1)} %param.21, s32[1024]{0:T(1024)S(1)} %pad_clamp_fusion), kind=kCustom, calls=%fused_computation | custom fusion | bytes 1050624 | tf_op jit(solution)/shard_map/gather | solution.py:137
  11.7 5.0 %collective-permute-start.1 = (bf16[512,512]{1,0:T(8,128)(2,1)S(1)}, bf16[512,512]{1,0:T(8,128)(2,1)}, u32[]{:S(2)}, u32[]{:S(2)}) collective-permute-start(bf16[512,512]{1,0:T(8,128)(2,1)S(1)} %gather_fusion), channel_id=1, source_target_pairs={{1,0},{2,1},{3,2},{4,3},{5,4},{6,5},{7,6},{8,7},{9,8},{10,9},{11,1... | collective-permute-start | bytes 1572872 | tf_op jit(solution)/shard_map/ppermute | solution.py:21
  16.8 3.5 %gather_fusion.2 = s32[512]{0:T(512)S(1)} fusion(s32[512]{0:T(512)S(1)} %copy-done.1, s32[1024]{0:T(1024)S(1)} %pad_clamp_fusion), kind=kCustom, calls=%fused_computation.2 | custom fusion | bytes 6144 | tf_op jit(solution)/shard_map/gather | solution.py:138
  20.4 4.4 %collective-permute-start.3 = (bf16[512]{0:T(512)(128)(2,1)S(1)}, bf16[512]{0:T(512)(128)(2,1)S(1)}, u32[]{:S(2)}, u32[]{:S(2)}) collective-permute-start(bf16[512]{0:T(512)(128)(2,1)S(1)} %convert_element_type.70), channel_id=1, source_target_pairs={{1,0},{2,1},{3,2},{4,3},{5,4},{6,5},{7,6},{8,7},{9,8},{10,9},{11,1... | collective-permute-start | bytes 3080 | tf_op jit(solution)/shard_map/ppermute | solution.py:21
  24.8 2.3 %convolution_convert_fusion.4 = bf16[512,512]{0,1:T(8,128)(2,1)} fusion(bf16[512,512]{1,0:T(8,128)(2,1)S(1)} %gather_fusion, bf16[512,512]{1,0:T(8,128)(2,1)} %param.25), kind=kOutput, calls=%fused_computation.52 | convolution fusion | flops 268697600 | bytes 1572864 | tf_op jit(solution)/shard_map/dot_general | solution.py:39
  27.3 3.5 %gather_fusion.1 = s32[512]{0:T(512)S(1)} fusion(s32[512]{0:T(512)S(1)} %copy-done.2, s32[1024]{0:T(1024)S(1)} %pad_clamp_fusion), kind=kCustom, calls=%fused_computation.1 | custom fusion | bytes 6144 | tf_op jit(solution)/shard_map/gather | solution.py:139
  30.9 2.5 %fusion.21 = pred[512,1536]{1,0:T(8,128)(4,1)} fusion(s32[512]{0:T(512)S(1)} %gather_fusion.1, s32[512]{0:T(512)S(1)} %iota_add_fusion, pred[1536]{0:T(1024)(128)(4,1)S(1)} %maximum_compare_fusion), kind=kLoop, calls=%fused_computation.39 | loop fusion | flops 4718592 | bytes 792064 | tf_op jit(solution)/shard_map/while/body/eval_jaxpr/and | solution.py:61
  35.6 3.3 %convolution_convert_fusion = bf16[1536,512]{0,1:T(8,128)(2,1)} fusion(bf16[1536,512]{1,0:T(8,128)(2,1)S(1)} %constant_dynamic-update-slice_fusion, bf16[512,512]{1,0:T(8,128)(2,1)} %param.26), kind=kOutput, calls=%fused_computation.41 | convolution fusion | flops 806092800 | bytes 3670016 | tf_op jit(solution)/shard_map/dot_general | solution.py:39
  38.9 2.2 %convolution_convert_fusion.1 = bf16[1536,512]{0,1:T(8,128)(2,1)} fusion(bf16[1536,512]{1,0:T(8,128)(2,1)S(1)} %constant_dynamic-update-slice_fusion, bf16[512,512]{1,0:T(8,128)(2,1)S(1)} %copy-done.11), kind=kOutput, calls=%fused_computation.42 | convolution fusion | flops 806092800 | bytes 3670016 | tf_op jit(solution)/shard_map/dot_general | solution.py:39
  41.1 16.0 %fusion.47 = (f32[8,512]{1,0:T(8,128)S(1)}, f32[8,512,1536]{2,1,0:T(8,128)}) fusion(pred[512,1536]{1,0:T(8,128)(4,1)S(1)} %copy-done.4, bf16[512,8,64]{0,2,1:T(8,128)(2,1)} %bitcast.90, bf16[1536,8,64]{0,2,1:T(8,128)(2,1)} %bitcast.97), kind=kOutput, calls=%fused_computation.87 | convolution fusion | flops 836765184 | bytes 28065792 | tf_op jit(solution)/shard_map/while/body/eval_jaxpr/sub | solution.py:64
  57.1 11.0 %fusion.32 = bf16[8,64,512]{2,1,0:T(8,128)(2,1)S(1)} fusion(bf16[1536,8,64]{0,2,1:T(8,128)(2,1)} %bitcast.96, f32[8,512,1536]{2,1,0:T(8,128)} %get-tuple-element.255, f32[8,512]{1,0:T(8,128)S(1)} %get-tuple-element.254), kind=kOutput, calls=%fused_computation.49 | convolution fusion | flops 818151424 | bytes 27279360 | tf_op jit(solution)/shard_map/while/body/eval_jaxpr/hqk,khd->qhd/dot_general | solution.py:66
  69.6 6.4 %multiply_reduce_fusion = (f32[512]{0:T(512)S(1)}, f32[512,512]{0,1:T(8,128)}) fusion(f32[512]{0:T(512)S(1)} %copy-done.12, f32[512,512]{0,1:T(8,128)} %get-tuple-element.257, f32[512]{0:T(512)S(1)} %add_rsqrt_fusion.1, bf16[2048,512]{1,0:T(8,128)(2,1)S(1)} %copy-done, bf16[512,2048]{1,0:T(8,128)(2,1)} %param.30), kind=kOutput, calls=%fused_computation.57 | convolution fusion | flops 2159541760 | bytes 6297600 | tf_op jit(solution)/shard_map/dot_general | solution.py:78
  77.4 2.5 %convolution_convert_fusion.3 = bf16[512,512]{1,0:T(8,128)(2,1)} fusion(bf16[512,512]{0,1:T(8,128)(2,1)S(1)} %multiply_convert_fusion, bf16[512,512]{1,0:T(8,128)(2,1)} %param.35), kind=kOutput, calls=%fused_computation.51 | convolution fusion | flops 268697600 | bytes 1572864 | tf_op jit(solution)/shard_map/dot_general | solution.py:39
  80.0 2.4 %convolution_convert_fusion.2 = bf16[512,512]{1,0:T(8,128)(2,1)} fusion(bf16[512,512]{0,1:T(8,128)(2,1)S(1)} %multiply_convert_fusion, bf16[512,512]{1,0:T(8,128)(2,1)} %param.36), kind=kOutput, calls=%fused_computation.50 | convolution fusion | flops 268697600 | bytes 1572864 | tf_op jit(solution)/shard_map/dot_general | solution.py:39
  82.6 30.5 %all_gather.19 = bf16[128,512]{1,0:T(8,128)(2,1)S(1)} all-gather(bf16[16,512]{1,0:T(8,128)(2,1)S(1)} %convolution_convert_fusion.6), channel_id=1, replica_groups=mesh['groups'=2,'hit'=8,'query'=2] {'hit'}, dimensions={0}, use_global_device_ids=true | all-gather | bytes 147456 | tf_op jit(solution)/shard_map/all_gather | solution.py:162
  113.3 1.5 copy.38
  114.8 2.8 %bitcast_reduce_fusion = (f32[128,8]{0,1:T(8,128)S(1)}, f32[8,1024,128]{2,1,0:T(8,128)}) fusion(bf16[1024,8,64]{0,2,1:T(8,128)(2,1)S(1)} %bitcast.87, bf16[128,8,64]{0,2,1:T(8,128)(2,1)S(1)} %bitcast.91), kind=kOutput, calls=%fused_computation.32 | convolution fusion | flops 136313856 | bytes 5378048 | tf_op jit(solution)/shard_map/while/body/eval_jaxpr/qhd,khd->qhk/dot_general | solution.py:91
  119.1 3.0 %fusion.23 = f32[8,64,128]{2,1,0:T(8,128)S(1)} fusion(bf16[1024,8,64]{0,2,1:T(8,128)(2,1)S(1)} %bitcast.88, f32[8,1024,128]{2,1,0:T(8,128)} %get-tuple-element.261, f32[128,8]{0,1:T(8,128)S(1)} %get-tuple-element.260), kind=kOutput, calls=%fused_computation.43 | convolution fusion | flops 137363456 | bytes 5509120 | tf_op jit(solution)/shard_map/while/body/eval_jaxpr/qhk,khd->qhd/dot_general | solution.py:98
  123.0 2.0 copy.45
  125.1 2.9 %fusion.19 = f32[128,8]{0,1:T(8,128)S(1)} fusion(f32[8,1024,128]{2,1,0:T(8,128)} %get-tuple-element.261, f32[128,8]{0,1:T(8,128)S(1)} %get-tuple-element.260), kind=kLoop, calls=%fused_computation.35 | loop fusion | flops 3144704 | bytes 4202496 | tf_op jit(solution)/shard_map/while/body/eval_jaxpr/reduce_sum | solution.py:96
  127.9 31.0 %all-gather.1 = f32[1024,8]{0,1:T(8,128)S(1)} all-gather(f32[128,8]{0,1:T(8,128)S(1)} %fusion.19), channel_id=3, replica_groups=mesh['groups'=2,'hit'=8,'query'=2] {'hit'}, dimensions={0}, use_global_device_ids=true | all-gather | bytes 36864 | tf_op jit(solution)/shard_map/all_gather | solution.py:29
  159.0 30.8 %all-gather = f32[1024,8]{0,1:T(8,128)S(1)} all-gather(f32[128,8]{0,1:T(8,128)S(1)} %get-tuple-element.260), channel_id=2, replica_groups=mesh['groups'=2,'hit'=8,'query'=2] {'hit'}, dimensions={0}, use_global_device_ids=true | all-gather | bytes 36864 | tf_op jit(solution)/shard_map/all_gather | solution.py:29
  190.9 8.8 %while.12 = (s32[]{:T(128)}, f32[128,8]{0,1:T(8,128)S(1)}, f32[128,8]{0,1:T(8,128)S(1)}, f32[128,512]{0,1:T(8,128)S(1)}, f32[8,128,8]{1,2,0:T(8,128)S(1)}, /*ind...) while((s32[]{:T(128)}, f32[128,8]{0,1:T(8,128)S(1)}, ...), condition=%wide.region_7.8_spmd, body=%wide.region_6.7_spmd.sunk | while | flops 202757 | bytes 1876119 | solution.py:35
  200.3 1.9 convolution_convert_fusion.5
  (94 shorter events, 19.8 us)
Async XLA Ops:
  7.2 62.4 %copy-start = (bf16[2048,512]{1,0:T(8,128)(2,1)S(1)}, bf16[2048,512]{1,0:T(8,128)(2,1)}, u32[]{:S(2)}) copy-start(bf16[2048,512]{1,0:T(8,128)(2,1)} %param.31) | copy-start | bytes 6291460
  7.2 9.6 %copy-start.1 = (s32[512]{0:T(512)S(1)}, s32[512]{0:T(512)}, u32[]{:S(2)}) copy-start(s32[512]{0:T(512)} %param.23) | copy-start | bytes 6148
  7.2 106.1 %all-gather.6.cloned.1.call-start = ((), (), s32[]{:S(2)}) async-start(), calls=%async_computation | async-start | bytes 1572864 | tf_op jit(solution)/shard_map/all_gather | solution.py:159
  8.1 19.3 %copy-start.2 = (s32[512]{0:T(512)S(1)}, s32[512]{0:T(512)}, u32[]{:S(2)}) copy-start(s32[512]{0:T(512)} %param.24) | copy-start | bytes 6148
  11.2 22.2 %collective-permute-start = (bf16[512,512]{1,0:T(8,128)(2,1)S(1)}, bf16[512,512]{1,0:T(8,128)(2,1)}, u32[]{:S(2)}, u32[]{:S(2)}) collective-permute-start(bf16[512,512]{1,0:T(8,128)(2,1)S(1)} %gather_fusion), channel_id=1, source_target_pairs={{0,1},{1,2},{2,3},{3,4},{4,5},{5,6},{6,7},{7,8},{8,9},{9,10},{10,1... | collective-permute-start | bytes 1572872 | tf_op jit(solution)/shard_map/ppermute | solution.py:19
  11.7 22.8 %collective-permute-start.1 = (bf16[512,512]{1,0:T(8,128)(2,1)S(1)}, bf16[512,512]{1,0:T(8,128)(2,1)}, u32[]{:S(2)}, u32[]{:S(2)}) collective-permute-start(bf16[512,512]{1,0:T(8,128)(2,1)S(1)} %gather_fusion), channel_id=1, source_target_pairs={{1,0},{2,1},{3,2},{4,3},{5,4},{6,5},{7,6},{8,7},{9,8},{10,9},{11,1... | collective-permute-start | bytes 1572872 | tf_op jit(solution)/shard_map/ppermute | solution.py:21
  20.3 10.5 %collective-permute-start.2 = (bf16[512]{0:T(512)(128)(2,1)S(1)}, bf16[512]{0:T(512)(128)(2,1)S(1)}, u32[]{:S(2)}, u32[]{:S(2)}) collective-permute-start(bf16[512]{0:T(512)(128)(2,1)S(1)} %convert_element_type.70), channel_id=1, source_target_pairs={{0,1},{1,2},{2,3},{3,4},{4,5},{5,6},{6,7},{7,8},{8,9},{9,10},{10,1... | collective-permute-start | bytes 3080 | tf_op jit(solution)/shard_map/ppermute | solution.py:19
  20.4 10.5 %collective-permute-start.3 = (bf16[512]{0:T(512)(128)(2,1)S(1)}, bf16[512]{0:T(512)(128)(2,1)S(1)}, u32[]{:S(2)}, u32[]{:S(2)}) collective-permute-start(bf16[512]{0:T(512)(128)(2,1)S(1)} %convert_element_type.70), channel_id=1, source_target_pairs={{1,0},{2,1},{3,2},{4,3},{5,4},{6,5},{7,6},{8,7},{9,8},{10,9},{11,1... | collective-permute-start | bytes 3080 | tf_op jit(solution)/shard_map/ppermute | solution.py:21
  30.9 8.1 %copy-start.11 = (bf16[512,512]{1,0:T(8,128)(2,1)S(1)}, bf16[512,512]{1,0:T(8,128)(2,1)}, u32[]{:S(2)}) copy-start(bf16[512,512]{1,0:T(8,128)(2,1)} %param.27) | copy-start | bytes 1572868
  35.6 5.5 %copy-start.4 = (pred[512,1536]{1,0:T(8,128)(4,1)S(1)}, pred[512,1536]{1,0:T(8,128)(4,1)}, u32[]{:S(2)}) copy-start(pred[512,1536]{1,0:T(8,128)(4,1)} %fusion.21) | copy-start | bytes 2359300
  57.1 11.0 %copy-start.7 = (bf16[512,512]{1,0:T(8,128)(2,1)S(1)}, bf16[512,512]{1,0:T(8,128)(2,1)}, u32[]{:S(2)}) copy-start(bf16[512,512]{1,0:T(8,128)(2,1)} %param.28) | copy-start | bytes 1572868
  57.1 12.5 %copy-start.12 = (f32[512]{0:T(512)S(1)}, f32[512]{0:T(512)}, u32[]{:S(2)}) copy-start(f32[512]{0:T(512)} %param.29) | copy-start | bytes 6148
  69.6 6.4 %copy-start.9 = (f32[512]{0:T(512)S(1)}, f32[512]{0:T(512)}, u32[]{:S(2)}) copy-start(f32[512]{0:T(512)} %param.32) | copy-start | bytes 6148
  76.0 6.5 %copy-start.6 = (bf16[512,512]{1,0:T(8,128)(2,1)S(1)}, bf16[512,512]{1,0:T(8,128)(2,1)}, u32[]{:S(2)}) copy-start(bf16[512,512]{1,0:T(8,128)(2,1)} %param.34) | copy-start | bytes 1572868
  76.0 6.5 %copy-start.8 = (bf16[16,512]{1,0:T(8,128)(2,1)S(1)}, bf16[16,512]{1,0:T(8,128)(2,1)}, u32[]{:S(2)}) copy-start(bf16[16,512]{1,0:T(8,128)(2,1)} %param.33) | copy-start | bytes 49156
  77.4 35.9 %copy-start.3 = (bf16[512,512]{0,1:T(8,128)(2,1)}, bf16[512,512]{0,1:T(8,128)(2,1)S(1)}, u32[]{:S(2)}) copy-start(bf16[512,512]{0,1:T(8,128)(2,1)S(1)} %multiply_convert_fusion) | copy-start | bytes 1572868
  80.0 37.6 %all-gather.8.cloned.1.call-start = ((), (), s32[]{:S(2)}) async-start(), calls=%async_computation.1 | async-start | bytes 1572864 | tf_op jit(solution)/shard_map/all_gather | solution.py:160
  82.4 107.3 %all-gather.10.cloned.1.call-start = ((), (), s32[]{:S(2)}) async-start(), calls=%async_computation.2 | async-start | bytes 2359296 | tf_op jit(solution)/shard_map/all_gather | solution.py:29
  190.8 9.1 %copy-start.5 = (bf16[512,512]{1,0:T(8,128)(2,1)S(1)}, bf16[512,512]{1,0:T(8,128)(2,1)}, u32[]{:S(2)}) copy-start(bf16[512,512]{1,0:T(8,128)(2,1)} %param.37) | copy-start | bytes 1572868
  190.9 9.4 %copy-start.10 = (f32[512]{0:T(512)S(1)}, f32[512]{0:T(512)}, u32[]{:S(2)}) copy-start(f32[512]{0:T(512)} %param.38) | copy-start | bytes 6148
Sparse Core Ops, SparseCore 0:
  80.1 6.6 all-gather.5
  88.3 10.1 all-gather.7
  123.1 47.2 all-gather.9
where the time goes:
time: 210 us; the launch traced here: 209 us
  blocking collectives  92.3 us (44%)
  matrix products  55.6 us (26%)
  local copies, waits for them, and re-layouts  27.4 us (13%)
  between operations  14.1 us (7%)
  starting transfers between devices  10.2 us (5%)
  other arithmetic  8.66 us (4%)
    all_gather x2, blocking collectives, joined(): everything = jax.tree.map(lambda part: lax.all_gather(part, axis), value)  61.8 us
    all_gather x1, blocking collectives, on_device(): all_queries = lax.all_gather(local_queries, 'hit', axis=0, tiled=True)  30.5 us
    sub x1, matrix products, band_attention(): expo = jnp.where(allowed[None], jnp.exp(scores - peak), 0.0)  16 us
    dot_general x6, matrix products, project(): jnp.dot(rows, weight, preferred_element_type=jnp.float32)  12.8 us
    dot_general x1, matrix products, band_attention(): jnp.einsum('hqk,khd->qhd', probs, value_heads, preferred_element_type=jnp...  11 us
    ppermute x2, starting transfers between devices, padded(): lax.ppermute(head, axis, [((i + 1) % count, i) for i in range(count)])  9.48 us
    dynamic_slice x14, local copies, waits for them, and re-layouts, lap(): return combine(so_far, jax.tree.map(lambda part: part[k], everything))  7.72 us
    dot_general x1, matrix products, encoder_tail(): jnp.dot(hidden, ffn_down, preferred_element_type=jnp.float32)  6.36 us
  transfers between devices with their start and end apart: 7, of which 0 were waited for; matrix products, arithmetic and copies ran while one was open for 12% of the time, Pallas kernels for 0%

commit v1 on v0

--- a/solution.py
+++ b/solution.py
@@ -159,7 +159,9 @@
         lax.all_gather(project(encoded, dec_wk), "query", axis=0, tiled=True),
         lax.all_gather(project(encoded, dec_wv), "query", axis=0, tiled=True),
     )
-    all_queries = lax.all_gather(local_queries, "hit", axis=0, tiled=True)
+    all_queries = jnp.concatenate(
+        lax.all_to_all(jnp.stack([local_queries] * lax.axis_size("hit")), "hit", 0, 0), axis=0
+    )
     count = all_queries.shape[0]
     qblock = 512 if count % 512 == 0 else count
 

time: 210 us -> 191 us (0.910)
  blocking collectives: 92.3 us -> 72 us
    all_gather x1 -> x0, blocking collectives: 30.5 us -> none  [on_device(): all_queries = lax.all_gather(local_queries, 'hit', axis=0, tiled=True)]
    all_to_all x0 -> x1, blocking collectives: none -> 9.74 us  [on_device(): lax.all_to_all(jnp.stack([local_queries] * lax.axis_size('hit')), 'hit',...]
  transfers between devices with their start and end apart: 7 -> 7, of which waited for: 0 -> 1; matrix products, arithmetic and copies ran while one was open for 12% -> 13% of each run, Pallas kernels for 0% -> 0%
where the time goes in v1:
time: 191 us; the launch traced here: 190 us
  blocking collectives  72 us (38%)
  matrix products  55.7 us (29%)
  local copies, waits for them, and re-layouts  27.5 us (14%)
  between operations  14.1 us (7%)
  starting transfers between devices  10.2 us (5%)
  other arithmetic  8.66 us (5%)
    all_gather x2, blocking collectives, joined(): everything = jax.tree.map(lambda part: lax.all_gather(part, axis), value)  62.3 us
    sub x1, matrix products, band_attention(): expo = jnp.where(allowed[None], jnp.exp(scores - peak), 0.0)  16 us
    dot_general x6, matrix products, project(): jnp.dot(rows, weight, preferred_element_type=jnp.float32)  12.8 us
    dot_general x1, matrix products, band_attention(): jnp.einsum('hqk,khd->qhd', probs, value_heads, preferred_element_type=jnp...  11 us
    all_to_all x1, blocking collectives, on_device(): lax.all_to_all(jnp.stack([local_queries] * lax.axis_size('hit')), 'hit',...  9.74 us
    ppermute x2, starting transfers between devices, padded(): lax.ppermute(head, axis, [((i + 1) % count, i) for i in range(count)])  9.48 us
    dynamic_slice x14, local copies, waits for them, and re-layouts, lap(): return combine(so_far, jax.tree.map(lambda part: part[k], everything))  7.72 us
    dot_general x1, matrix products, encoder_tail(): jnp.dot(hidden, ffn_down, preferred_element_type=jnp.float32)  6.36 us
  transfers between devices with their start and end apart: 7, of which 1 were waited for; matrix products, arithmetic and copies ran while one was open for 13% of the time, Pallas kernels for 0%

profile of v1, /device:TPU:0, one launch (start us, length us, event | category | flops | bytes accessed | tf_op | source)
XLA Modules:
  0.0 190.1 jit_solution(2230931386898895571)
XLA Ops:
  8.1 3.1 %gather_fusion = bf16[512,512]{1,0:T(8,128)(2,1)S(1)} fusion(bf16[512,512]{1,0:T(8,128)(2,1)} %param.21, s32[1024]{0:T(1024)S(1)} %pad_clamp_fusion), kind=kCustom, calls=%fused_computation | custom fusion | bytes 1050624 | tf_op jit(solution)/shard_map/gather | solution.py:137
  11.7 5.0 %collective-permute-start.1 = (bf16[512,512]{1,0:T(8,128)(2,1)S(1)}, bf16[512,512]{1,0:T(8,128)(2,1)}, u32[]{:S(2)}, u32[]{:S(2)}) collective-permute-start(bf16[512,512]{1,0:T(8,128)(2,1)S(1)} %gather_fusion), channel_id=1, source_target_pairs={{1,0},{2,1},{3,2},{4,3},{5,4},{6,5},{7,6},{8,7},{9,8},{10,9},{11,1... | collective-permute-start | bytes 1572872 | tf_op jit(solution)/shard_map/ppermute | solution.py:21
  16.8 3.5 %gather_fusion.2 = s32[512]{0:T(512)S(1)} fusion(s32[512]{0:T(512)S(1)} %copy-done.1, s32[1024]{0:T(1024)S(1)} %pad_clamp_fusion), kind=kCustom, calls=%fused_computation.2 | custom fusion | bytes 6144 | tf_op jit(solution)/shard_map/gather | solution.py:138
  20.4 4.4 %collective-permute-start.3 = (bf16[512]{0:T(512)(128)(2,1)S(1)}, bf16[512]{0:T(512)(128)(2,1)S(1)}, u32[]{:S(2)}, u32[]{:S(2)}) collective-permute-start(bf16[512]{0:T(512)(128)(2,1)S(1)} %convert_element_type.70), channel_id=1, source_target_pairs={{1,0},{2,1},{3,2},{4,3},{5,4},{6,5},{7,6},{8,7},{9,8},{10,9},{11,1... | collective-permute-start | bytes 3080 | tf_op jit(solution)/shard_map/ppermute | solution.py:21
  24.8 2.3 %convolution_convert_fusion.4 = bf16[512,512]{0,1:T(8,128)(2,1)} fusion(bf16[512,512]{1,0:T(8,128)(2,1)S(1)} %gather_fusion, bf16[512,512]{1,0:T(8,128)(2,1)} %param.25), kind=kOutput, calls=%fused_computation.52 | convolution fusion | flops 268697600 | bytes 1572864 | tf_op jit(solution)/shard_map/dot_general | solution.py:39
  27.3 3.5 %gather_fusion.1 = s32[512]{0:T(512)S(1)} fusion(s32[512]{0:T(512)S(1)} %copy-done.2, s32[1024]{0:T(1024)S(1)} %pad_clamp_fusion), kind=kCustom, calls=%fused_computation.1 | custom fusion | bytes 6144 | tf_op jit(solution)/shard_map/gather | solution.py:139
  30.9 2.5 %fusion.21 = pred[512,1536]{1,0:T(8,128)(4,1)} fusion(s32[512]{0:T(512)S(1)} %gather_fusion.1, s32[512]{0:T(512)S(1)} %iota_add_fusion, pred[1536]{0:T(1024)(128)(4,1)S(1)} %maximum_compare_fusion), kind=kLoop, calls=%fused_computation.39 | loop fusion | flops 4718592 | bytes 792064 | tf_op jit(solution)/shard_map/while/body/eval_jaxpr/and | solution.py:61
  35.6 3.3 %convolution_convert_fusion = bf16[1536,512]{0,1:T(8,128)(2,1)} fusion(bf16[1536,512]{1,0:T(8,128)(2,1)S(1)} %constant_dynamic-update-slice_fusion, bf16[512,512]{1,0:T(8,128)(2,1)} %param.26), kind=kOutput, calls=%fused_computation.41 | convolution fusion | flops 806092800 | bytes 3670016 | tf_op jit(solution)/shard_map/dot_general | solution.py:39
  38.9 2.2 %convolution_convert_fusion.1 = bf16[1536,512]{0,1:T(8,128)(2,1)} fusion(bf16[1536,512]{1,0:T(8,128)(2,1)S(1)} %constant_dynamic-update-slice_fusion, bf16[512,512]{1,0:T(8,128)(2,1)S(1)} %copy-done.11), kind=kOutput, calls=%fused_computation.42 | convolution fusion | flops 806092800 | bytes 3670016 | tf_op jit(solution)/shard_map/dot_general | solution.py:39
  41.1 16.0 %fusion.49 = (f32[8,512]{1,0:T(8,128)S(1)}, f32[8,512,1536]{2,1,0:T(8,128)}) fusion(pred[512,1536]{1,0:T(8,128)(4,1)S(1)} %copy-done.4, bf16[512,8,64]{0,2,1:T(8,128)(2,1)} %bitcast.88, bf16[1536,8,64]{0,2,1:T(8,128)(2,1)} %bitcast.94), kind=kOutput, calls=%fused_computation.89 | convolution fusion | flops 836765184 | bytes 28065792 | tf_op jit(solution)/shard_map/while/body/eval_jaxpr/sub | solution.py:64
  57.1 11.0 %fusion.32 = bf16[8,64,512]{2,1,0:T(8,128)(2,1)S(1)} fusion(bf16[1536,8,64]{0,2,1:T(8,128)(2,1)} %bitcast.93, f32[8,512,1536]{2,1,0:T(8,128)} %get-tuple-element.255, f32[8,512]{1,0:T(8,128)S(1)} %get-tuple-element.254), kind=kOutput, calls=%fused_computation.49 | convolution fusion | flops 818151424 | bytes 27279360 | tf_op jit(solution)/shard_map/while/body/eval_jaxpr/hqk,khd->qhd/dot_general | solution.py:66
  69.6 6.4 %multiply_reduce_fusion = (f32[512]{0:T(512)S(1)}, f32[512,512]{0,1:T(8,128)}) fusion(f32[512]{0:T(512)S(1)} %copy-done.12, f32[512,512]{0,1:T(8,128)} %get-tuple-element.257, f32[512]{0:T(512)S(1)} %add_rsqrt_fusion.1, bf16[2048,512]{1,0:T(8,128)(2,1)S(1)} %copy-done, bf16[512,2048]{1,0:T(8,128)(2,1)} %param.30), kind=kOutput, calls=%fused_computation.57 | convolution fusion | flops 2159541760 | bytes 6297600 | tf_op jit(solution)/shard_map/dot_general | solution.py:78
  77.4 2.5 %convolution_convert_fusion.3 = bf16[512,512]{1,0:T(8,128)(2,1)} fusion(bf16[512,512]{0,1:T(8,128)(2,1)S(1)} %multiply_convert_fusion, bf16[512,512]{1,0:T(8,128)(2,1)} %param.35), kind=kOutput, calls=%fused_computation.51 | convolution fusion | flops 268697600 | bytes 1572864 | tf_op jit(solution)/shard_map/dot_general | solution.py:39
  80.0 2.4 %convolution_convert_fusion.2 = bf16[512,512]{1,0:T(8,128)(2,1)} fusion(bf16[512,512]{0,1:T(8,128)(2,1)S(1)} %multiply_convert_fusion, bf16[512,512]{1,0:T(8,128)(2,1)} %param.36), kind=kOutput, calls=%fused_computation.50 | convolution fusion | flops 268697600 | bytes 1572864 | tf_op jit(solution)/shard_map/dot_general | solution.py:39
  82.7 9.7 %all_to_all.5 = bf16[8,16,512]{2,1,0:T(8,128)(2,1)S(1)} all-to-all(bf16[8,16,512]{2,1,0:T(8,128)(2,1)S(1)} %stack.2), channel_id=1, replica_groups=mesh['groups'=2,'hit'=8,'query'=2] {'hit'}, dimensions={0} | all-to-all | bytes 262144 | tf_op jit(solution)/shard_map/all_to_all | solution.py:163
  94.1 2.8 %bitcast_reduce_fusion = (f32[128,8]{0,1:T(8,128)S(1)}, f32[8,1024,128]{2,1,0:T(8,128)}) fusion(bf16[1024,8,64]{0,2,1:T(8,128)(2,1)S(1)} %bitcast.85, bf16[128,8,64]{2,1,0:T(8,128)(2,1)S(1)} %reshape_reshape.4), kind=kOutput, calls=%fused_computation.32 | convolution fusion | flops 136313856 | bytes 5378048 | tf_op jit(solution)/shard_map/while/body/eval_jaxpr/qhd,khd->qhk/dot_general | solution.py:91
  96.9 1.6 all-gather.8.cloned.1.call-done
  100.1 3.0 %fusion.23 = f32[8,64,128]{2,1,0:T(8,128)S(1)} fusion(bf16[1024,8,64]{0,2,1:T(8,128)(2,1)S(1)} %bitcast.86, f32[8,1024,128]{2,1,0:T(8,128)} %get-tuple-element.261, f32[128,8]{0,1:T(8,128)S(1)} %get-tuple-element.260), kind=kOutput, calls=%fused_computation.43 | convolution fusion | flops 137363456 | bytes 5509120 | tf_op jit(solution)/shard_map/while/body/eval_jaxpr/qhk,khd->qhd/dot_general | solution.py:98
  104.0 2.0 %copy.45 = bf16[512,512]{1,0:T(8,128)(2,1)} copy(bf16[512,512]{0,1:T(8,128)(2,1)} %copy-done.3) | data formatting | bytes 1048576
  106.0 2.9 %fusion.19 = f32[128,8]{0,1:T(8,128)S(1)} fusion(f32[8,1024,128]{2,1,0:T(8,128)} %get-tuple-element.261, f32[128,8]{0,1:T(8,128)S(1)} %get-tuple-element.260), kind=kLoop, calls=%fused_computation.35 | loop fusion | flops 3144704 | bytes 4202496 | tf_op jit(solution)/shard_map/while/body/eval_jaxpr/reduce_sum | solution.py:96
  108.9 31.5 %all-gather.1 = f32[1024,8]{0,1:T(8,128)S(1)} all-gather(f32[128,8]{0,1:T(8,128)S(1)} %fusion.19), channel_id=3, replica_groups=mesh['groups'=2,'hit'=8,'query'=2] {'hit'}, dimensions={0}, use_global_device_ids=true | all-gather | bytes 36864 | tf_op jit(solution)/shard_map/all_gather | solution.py:29
  140.4 30.8 %all-gather = f32[1024,8]{0,1:T(8,128)S(1)} all-gather(f32[128,8]{0,1:T(8,128)S(1)} %get-tuple-element.260), channel_id=2, replica_groups=mesh['groups'=2,'hit'=8,'query'=2] {'hit'}, dimensions={0}, use_global_device_ids=true | all-gather | bytes 36864 | tf_op jit(solution)/shard_map/all_gather | solution.py:29
  172.3 8.8 %while.12 = (s32[]{:T(128)}, f32[128,8]{0,1:T(8,128)S(1)}, f32[128,8]{0,1:T(8,128)S(1)}, f32[128,512]{0,1:T(8,128)S(1)}, f32[8,128,8]{1,2,0:T(8,128)S(1)}, /*ind...) while((s32[]{:T(128)}, f32[128,8]{0,1:T(8,128)S(1)}, ...), condition=%wide.region_7.8_spmd, body=%wide.region_6.7_spmd.sunk | while | flops 202757 | bytes 1876119 | solution.py:35
  181.7 1.9 convolution_convert_fusion.5
  (95 shorter events, 21.4 us)
Async XLA Ops:
  7.2 62.4 %copy-start = (bf16[2048,512]{1,0:T(8,128)(2,1)S(1)}, bf16[2048,512]{1,0:T(8,128)(2,1)}, u32[]{:S(2)}) copy-start(bf16[2048,512]{1,0:T(8,128)(2,1)} %param.31) | copy-start | bytes 6291460
  7.2 9.6 %copy-start.1 = (s32[512]{0:T(512)S(1)}, s32[512]{0:T(512)}, u32[]{:S(2)}) copy-start(s32[512]{0:T(512)} %param.23) | copy-start | bytes 6148
  7.2 85.4 %all-gather.6.cloned.1.call-start = ((), (), s32[]{:S(2)}) async-start(), calls=%async_computation.1 | async-start | bytes 1572864 | tf_op jit(solution)/shard_map/all_gather | solution.py:159
  8.1 19.3 %copy-start.2 = (s32[512]{0:T(512)S(1)}, s32[512]{0:T(512)}, u32[]{:S(2)}) copy-start(s32[512]{0:T(512)} %param.24) | copy-start | bytes 6148
  11.2 22.2 %collective-permute-start = (bf16[512,512]{1,0:T(8,128)(2,1)S(1)}, bf16[512,512]{1,0:T(8,128)(2,1)}, u32[]{:S(2)}, u32[]{:S(2)}) collective-permute-start(bf16[512,512]{1,0:T(8,128)(2,1)S(1)} %gather_fusion), channel_id=1, source_target_pairs={{0,1},{1,2},{2,3},{3,4},{4,5},{5,6},{6,7},{7,8},{8,9},{9,10},{10,1... | collective-permute-start | bytes 1572872 | tf_op jit(solution)/shard_map/ppermute | solution.py:19
  11.7 22.8 %collective-permute-start.1 = (bf16[512,512]{1,0:T(8,128)(2,1)S(1)}, bf16[512,512]{1,0:T(8,128)(2,1)}, u32[]{:S(2)}, u32[]{:S(2)}) collective-permute-start(bf16[512,512]{1,0:T(8,128)(2,1)S(1)} %gather_fusion), channel_id=1, source_target_pairs={{1,0},{2,1},{3,2},{4,3},{5,4},{6,5},{7,6},{8,7},{9,8},{10,9},{11,1... | collective-permute-start | bytes 1572872 | tf_op jit(solution)/shard_map/ppermute | solution.py:21
  20.3 10.5 %collective-permute-start.2 = (bf16[512]{0:T(512)(128)(2,1)S(1)}, bf16[512]{0:T(512)(128)(2,1)S(1)}, u32[]{:S(2)}, u32[]{:S(2)}) collective-permute-start(bf16[512]{0:T(512)(128)(2,1)S(1)} %convert_element_type.70), channel_id=1, source_target_pairs={{0,1},{1,2},{2,3},{3,4},{4,5},{5,6},{6,7},{7,8},{8,9},{9,10},{10,1... | collective-permute-start | bytes 3080 | tf_op jit(solution)/shard_map/ppermute | solution.py:19
  20.4 10.5 %collective-permute-start.3 = (bf16[512]{0:T(512)(128)(2,1)S(1)}, bf16[512]{0:T(512)(128)(2,1)S(1)}, u32[]{:S(2)}, u32[]{:S(2)}) collective-permute-start(bf16[512]{0:T(512)(128)(2,1)S(1)} %convert_element_type.70), channel_id=1, source_target_pairs={{1,0},{2,1},{3,2},{4,3},{5,4},{6,5},{7,6},{8,7},{9,8},{10,9},{11,1... | collective-permute-start | bytes 3080 | tf_op jit(solution)/shard_map/ppermute | solution.py:21
  30.9 8.1 %copy-start.11 = (bf16[512,512]{1,0:T(8,128)(2,1)S(1)}, bf16[512,512]{1,0:T(8,128)(2,1)}, u32[]{:S(2)}) copy-start(bf16[512,512]{1,0:T(8,128)(2,1)} %param.27) | copy-start | bytes 1572868
  35.6 5.5 %copy-start.4 = (pred[512,1536]{1,0:T(8,128)(4,1)S(1)}, pred[512,1536]{1,0:T(8,128)(4,1)}, u32[]{:S(2)}) copy-start(pred[512,1536]{1,0:T(8,128)(4,1)} %fusion.21) | copy-start | bytes 2359300
  57.1 11.0 %copy-start.7 = (bf16[512,512]{1,0:T(8,128)(2,1)S(1)}, bf16[512,512]{1,0:T(8,128)(2,1)}, u32[]{:S(2)}) copy-start(bf16[512,512]{1,0:T(8,128)(2,1)} %param.28) | copy-start | bytes 1572868
  57.1 12.5 %copy-start.12 = (f32[512]{0:T(512)S(1)}, f32[512]{0:T(512)}, u32[]{:S(2)}) copy-start(f32[512]{0:T(512)} %param.29) | copy-start | bytes 6148
  69.6 6.4 %copy-start.9 = (f32[512]{0:T(512)S(1)}, f32[512]{0:T(512)}, u32[]{:S(2)}) copy-start(f32[512]{0:T(512)} %param.32) | copy-start | bytes 6148
  76.0 6.5 %copy-start.6 = (bf16[512,512]{1,0:T(8,128)(2,1)S(1)}, bf16[512,512]{1,0:T(8,128)(2,1)}, u32[]{:S(2)}) copy-start(bf16[512,512]{1,0:T(8,128)(2,1)} %param.34) | copy-start | bytes 1572868
  76.0 6.5 %copy-start.8 = (bf16[16,512]{1,0:T(8,128)(2,1)S(1)}, bf16[16,512]{1,0:T(8,128)(2,1)}, u32[]{:S(2)}) copy-start(bf16[16,512]{1,0:T(8,128)(2,1)} %param.33) | copy-start | bytes 49156
  77.4 15.2 %copy-start.3 = (bf16[512,512]{0,1:T(8,128)(2,1)}, bf16[512,512]{0,1:T(8,128)(2,1)S(1)}, u32[]{:S(2)}) copy-start(bf16[512,512]{0,1:T(8,128)(2,1)S(1)} %multiply_convert_fusion) | copy-start | bytes 1572868
  80.0 18.6 %all-gather.8.cloned.1.call-start = ((), (), s32[]{:S(2)}) async-start(), calls=%async_computation.2 | async-start | bytes 1572864 | tf_op jit(solution)/shard_map/all_gather | solution.py:160
  82.4 88.8 %all-gather.10.cloned.1.call-start = ((), (), s32[]{:S(2)}) async-start(), calls=%async_computation.3 | async-start | bytes 2359296 | tf_op jit(solution)/shard_map/all_gather | solution.py:29
  172.3 9.1 %copy-start.5 = (bf16[512,512]{1,0:T(8,128)(2,1)S(1)}, bf16[512,512]{1,0:T(8,128)(2,1)}, u32[]{:S(2)}) copy-start(bf16[512,512]{1,0:T(8,128)(2,1)} %param.37) | copy-start | bytes 1572868
  172.3 9.4 %copy-start.10 = (f32[512]{0:T(512)S(1)}, f32[512]{0:T(512)}, u32[]{:S(2)}) copy-start(f32[512]{0:T(512)} %param.38) | copy-start | bytes 6148
Sparse Core Ops, SparseCore 0:
  80.1 6.6 all-gather.5
  88.3 10.1 all-gather.7
  104.1 50.6 all-gather.9
